TPU v7x, 32 devices: a whole 2x2x4 slice. The times are simulated.
32 devices in a mesh: ia: 4 (over z), ja: 4 (over y, core), ka: 2 (over x).
Axes of the slice: x: 2, y: 2, z: 4, core: 2. Of those that a mesh axis runs over, the one named last changes fastest.
Arguments:
- tensor: float32 [8192, 8, 1024], P('ja', 'ka', 'ia'), may hold values from -6 to 6
- factor_a: float32 [1024, 128], P('ia'), may hold values from -1 to 1
- factor_c: float32 [8, 128], P('ka'), may hold values from -2 to 2
- gram_c: float32 [128, 128], replicated, may hold values from -12 to 24, as said below
Outputs:
- factor_b: float32 [8192, 128], P('ja')
- factor_c_new: float32 [8, 128], P('ka')
Inputs may be any that keep to these rules, and one draw needn't show every extreme that they name: `gram_c`: symmetric positive definite.
All inputs are finite; a program needn't handle non-finite values.
Results may differ from a plain program's by a relative error of at most 0.000071.
Values sent between devices are 32-bit elements; how exact they have to be, the bound alone decides.
A program may use at most 64 MiB of HBM per device.

v0:
```python
import jax
import jax.numpy as jnp
from jax import lax
from jax.sharding import PartitionSpec as P


def right_solve(rhs, system):
    lower = jnp.linalg.cholesky(system)
    middle = lax.linalg.triangular_solve(lower, rhs, left_side=False, lower=True, transpose_a=True)
    return lax.linalg.triangular_solve(
        lower, middle, left_side=False, lower=True, transpose_a=False
    )


def body(tensor, factor_a, factor_c, gram_c):
    high = lax.Precision.HIGHEST
    mode_two, mode_three, mode_one = tensor.shape
    rank = factor_a.shape[1]
    gram_a = lax.psum(
        jnp.dot(factor_a.T, factor_a, precision=high, preferred_element_type=jnp.float32), "ia"
    )
    system_b = gram_a * gram_c
    flat = jnp.dot(
        tensor.reshape(mode_two * mode_three, mode_one),
        factor_a,
        precision=high,
        preferred_element_type=jnp.float32,
    )
    partial_value = flat.reshape(mode_two, mode_three, rank)
    mttkrp_b = lax.psum(jnp.sum(partial_value * factor_c[None, :, :], axis=1), ("ia", "ka"))
    factor_b = right_solve(mttkrp_b, system_b)
    mttkrp_c = lax.psum(jnp.sum(partial_value * factor_b[:, None, :], axis=0), ("ia", "ja"))
    gram_b = lax.psum(
        jnp.dot(factor_b.T, factor_b, precision=high, preferred_element_type=jnp.float32), "ja"
    )
    factor_c_new = right_solve(mttkrp_c, gram_a * gram_b)
    return (factor_b, factor_c_new)


def solution(mesh):
    placed = (P("ja", "ka", "ia"), P("ia", None), P("ka", None), P())
    return jax.shard_map(
        body, mesh=mesh, in_specs=placed, out_specs=(P("ja", None), P("ka", None)), check_vma=False
    )
```

profile of v0, /device:TPU:0, one launch (start us, length us, event | category | flops | bytes accessed | tf_op | source)
XLA Modules:
  0.0 200.3 jit_solution(17277993881042223334)
XLA Ops:
  7.2 0.8 copy-done
  8.1 1.0 fusion.15
  9.2 12.6 %multiply_reduce_fusion.1 = (f32[2048,128]{1,0:T(8,128)}, f32[2048,4,128]{2,0,1:T(8,128)}) fusion(f32[4,128]{1,0:T(4,128)} %param.7, f32[256,128]{1,0:T(8,128)S(1)} %copy-done, f32[2048,4,256]{2,1,0:T(4,128)} %param.5), kind=kOutput, calls=%fused_computation.3 | convolution fusion | flops 3223060480 | bytes 13764608 | tf_op jit(solution)/shard_map/dot_general | solution.py:23
  21.8 0.2 all-reduce.8.cloned.1.call-start
  22.0 0.1 copy.8
  22.1 25.2 %all-reduce.6.cloned.1.call-done = f32[128,128]{0,1:T(8,128)} async-done(((f32[128,128]{0,1:T(8,128)}), f32[128,128]{0,1:T(8,128)}) %all-reduce.6.cloned.1.call-update) | async-done | bytes 65552 | tf_op jit(solution)/shard_map/psum | solution.py:19
  47.3 0.8 mul.24
  48.3 11.7 %cholesky.44 = f32[128,128]{1,0:T(8,128)S(1)} custom-call(f32[128,128]{1,0:T(8,128)S(1)} %fusion.14), custom_call_target="Cholesky" | custom-call | tf_op jit(solution)/shard_map/jit(cholesky)/cholesky | solution.py:8
  60.1 0.6 compare_reduce_fusion.1
  60.7 0.7 fusion.3
  61.4 9.8 %custom-call.12 = f32[1,128,128]{1,2,0:T(8,128)S(1)} custom-call(f32[1,128,128]{2,1,0:T(8,128)S(1)} %fusion.3), custom_call_target="InvertDiagBlocksLowerTriangular" | custom-call | tf_op jit(solution)/shard_map/triangular_solve | solution.py:9
  71.2 58.4 %all-reduce.4.cloned.1.call-done = f32[2048,128]{1,0:T(8,128)} async-done(((f32[2048,128]{1,0:T(8,128)}), f32[2048,128]{1,0:T(8,128)}) %all-reduce.4.cloned.1.call-update) | async-done | bytes 1048592 | tf_op jit(solution)/shard_map/psum | solution.py:30
  129.6 2.2 %fusion.12 = f32[2048,128]{1,0:T(8,128)S(1)} fusion(f32[2048,128]{1,0:T(8,128)} %all-reduce.4.cloned.1.call-done, f32[1,128,128]{1,2,0:T(8,128)S(1)} %custom-call.12), kind=kOutput, calls=%fused_computation.17 | convolution fusion | flops 402653184 | bytes 2162688 | tf_op jit(solution)/shard_map/triangular_solve | solution.py:9
  131.8 1.0 fusion.10
  132.8 2.4 %fusion.16 = f32[128,128]{0,1:T(8,128)} fusion(f32[2048,128]{1,0:T(8,128)S(1)} %fusion.10), kind=kOutput, calls=%fused_computation.28 | convolution fusion | flops 402653184 | bytes 1114112 | tf_op jit(solution)/shard_map/dot_general | solution.py:34
  135.2 2.5 %multiply_reduce_fusion = f32[4,128]{1,0:T(4,128)S(1)} fusion(f32[2048,4,128]{2,0,1:T(8,128)} %get-tuple-element.4, f32[2048,128]{1,0:T(8,128)S(1)} %fusion.10), kind=kLoop, calls=%fused_computation.2 | loop fusion | flops 2096640 | bytes 5244928 | tf_op jit(solution)/shard_map/reduce_sum | solution.py:32
  137.7 31.2 %psum.30 = f32[4,128]{1,0:T(4,128)S(1)} all-reduce(f32[4,128]{1,0:T(4,128)S(1)} %multiply_reduce_fusion), channel_id=1, replica_groups=mesh['ia'=4,'ja'=4,'ka'=2] {'ia','ja'}, use_global_device_ids=true, to_apply=%region_6.8 | all-reduce | flops 512 | bytes 4096 | tf_op jit(solution)/shard_map/psum | solution.py:32
  169.0 0.8 mul.27
  169.9 11.7 %cholesky.55 = f32[128,128]{1,0:T(8,128)S(1)} custom-call(f32[128,128]{1,0:T(8,128)S(1)} %fusion.9), custom_call_target="Cholesky" | custom-call | tf_op jit(solution)/shard_map/jit(cholesky)/cholesky | solution.py:8
  181.7 0.6 compare_reduce_fusion
  182.3 0.7 fusion.4
  183.0 9.8 %custom-call.13 = f32[1,128,128]{1,2,0:T(8,128)S(1)} custom-call(f32[1,128,128]{2,1,0:T(8,128)S(1)} %fusion.4), custom_call_target="InvertDiagBlocksLowerTriangular" | custom-call | tf_op jit(solution)/shard_map/triangular_solve | solution.py:9
  192.8 0.2 fusion.7
  193.0 0.8 fusion.5
  (19 shorter events, 0.4 us)
Async XLA Ops:
  7.2 0.9 copy-start
  7.2 40.2 %all-reduce.6.cloned.1.call-start = ((), (), s32[]{:S(2)}) async-start(), calls=%async_computation.1 | async-start | bytes 131072 | tf_op jit(solution)/shard_map/psum | solution.py:19
  9.1 12.9 %copy-start.3 = (f32[128,128]{1,0:T(8,128)S(1)}, f32[128,128]{1,0:T(8,128)}, u32[]{:S(2)}) copy-start(f32[128,128]{1,0:T(8,128)} %param.8) | copy-start | bytes 196612
  9.1 120.5 %all-reduce.4.cloned.1.call-start = ((), (), s32[]{:S(2)}) async-start(), calls=%async_computation | async-start | bytes 2097152 | tf_op jit(solution)/shard_map/psum | solution.py:30
  21.8 147.2 %all-reduce.8.cloned.1.call-start = ((), (), s32[]{:S(2)}) async-start(), calls=%async_computation.2 | async-start | bytes 131072 | tf_op jit(solution)/shard_map/psum | solution.py:33
  132.8 61.0 %copy-start.1 = (f32[2048,128]{1,0:T(8,128)}, f32[2048,128]{1,0:T(8,128)S(1)}, u32[]{:S(2)}) copy-start(f32[2048,128]{1,0:T(8,128)S(1)} %fusion.10) | copy-start | bytes 3145732
  132.8 36.2 %copy-start.2 = (f32[128,128]{0,1:T(8,128)S(1)}, f32[128,128]{0,1:T(8,128)}, u32[]{:S(2)}) copy-start(f32[128,128]{0,1:T(8,128)} %all-reduce.6.cloned.1.call-done) | copy-start | bytes 196612
Sparse Core Ops, SparseCore 0:
  10.3 37.0 all-reduce.5
  51.4 78.1 all-reduce.3
  135.4 31.1 all-reduce.7
where the time goes:
time: 201 us; the launch traced here: 200 us
  waiting for transfers between devices  83.7 us (42%)
  other arithmetic  49.9 us (25%)
  blocking collectives  31.2 us (16%)
  matrix products  20.2 us (10%)
  between operations  13.9 us (7%)
    psum x1, waiting for transfers between devices, body(): lax.psum(jnp.sum(partial_value * factor_c[None, :, :], axis=1), ('ia', 'k...  58.4 us
    psum x1, blocking collectives, body(): lax.psum(jnp.sum(partial_value * factor_b[:, None, :], axis=0), ('ia', 'j...  31.2 us
    psum x1, waiting for transfers between devices, body(): lax.psum(jnp.dot(factor_a.T, factor_a, precision=high, preferred_element_...  25.2 us
    another operation x6, other arithmetic, right_solve(): lower = jnp.linalg.cholesky(system)  24.8 us
    another operation x4, other arithmetic, right_solve(): lax.linalg.triangular_solve(lower, rhs, left_side=False, lower=True, tran...  20.9 us
    dot_general x1, matrix products, body(): jnp.dot(tensor.reshape(mode_two * mode_three, mode_one), factor_a, precis...  12.6 us
  transfers between devices with their start and end apart: 3, of which 2 were waited for; matrix products, arithmetic and copies ran while one was open for 19% of the time, Pallas kernels for 0%

commit v1 on v0

v1 whole, which is shorter than its diff:
```python
import functools

import jax
import jax.numpy as jnp
from jax import lax
from jax.experimental import pallas as pl
from jax.experimental.pallas import tpu as pltpu
from jax.sharding import PartitionSpec as P

HIGH = lax.Precision.HIGHEST
MESH = pl.DeviceIdType.MESH
GROUP = 8


def mm(a, b):
    return jnp.dot(a, b, precision=HIGH, preferred_element_type=jnp.float32)


def mtm(a):
    return lax.dot_general(
        a, a, (((0,), (0,)), ((), ())), precision=HIGH, preferred_element_type=jnp.float32
    )


def eliminate(a):
    n = a.shape[0]
    lane = lax.broadcasted_iota(jnp.int32, (n, n), 1)
    sub = lax.broadcasted_iota(jnp.int32, (n, n), 0)
    lane_row = lax.broadcasted_iota(jnp.int32, (1, n), 1)
    for t in range(GROUP):
        col = jnp.broadcast_to(a[:, t : t + 1], (n, n))
        inv = 1.0 / col[t : t + 1, :]
        row = jnp.where(lane_row == t, inv, a[t : t + 1, :] * inv)
        a = jnp.where(sub == t, row, jnp.where(lane == t, 0.0, a) - col * row)
    a = pltpu.roll(a, n - GROUP, axis=1)
    return jnp.concatenate([a[GROUP:], a[:GROUP]], axis=0)


def kernel(
    dims,
    blocks,
    t_hbm,
    a_ref,
    c_ref,
    gc_ref,
    b_out,
    c_out,
    tbuf,
    part,
    mloc,
    xrecv,
    xsum,
    zrecv,
    bfull,
    ga_all,
    gb_all,
    mc_all,
    inv_ref,
    acc_ref,
    t_sem,
    x_send,
    x_recv,
    z_send,
    z_recv,
    p_send,
    p_recv,
    q_send,
    q_recv,
    ga_send,
    ga_recv,
    gb_send,
    gb_recv,
    mc_send,
    mc_recv,
    o_sem,
):
    ni, nj, nk = dims
    kl, rows, rank = part.shape
    jb = rows // blocks
    jx = jb // nk
    jz = jx // ni
    mi, mj, mk = lax.axis_index("ia"), lax.axis_index("ja"), lax.axis_index("ka")
    sends = []

    def peer(axis, me, n, d):
        return {axis: lax.rem(me + d, n)}

    def remote(src, dst, ss, rs, who):
        cp = pltpu.make_async_remote_copy(
            src_ref=src, dst_ref=dst, send_sem=ss, recv_sem=rs, device_id=who, device_id_type=MESH
        )
        cp.start()
        sends.append(cp)
        return cp

    tcopies = {}
    for b in range(blocks):
        for k in range(kl):
            rs = pl.ds(b * jb, jb)
            cp = pltpu.make_async_copy(t_hbm.at[rs, k, :], tbuf.at[k, rs, :], t_sem.at[b, k])
            cp.start()
            tcopies[b, k] = cp

    barrier = pltpu.get_barrier_semaphore()
    for axis, me, n in (("ia", mi, ni), ("ja", mj, nj), ("ka", mk, nk)):
        for d in range(1, n):
            pl.semaphore_signal(
                barrier, inc=1, device_id=peer(axis, me, n, d), device_id_type=MESH
            )

    a = a_ref[...]
    a_hi = a.astype(jnp.bfloat16)
    a_lo = (a - a_hi.astype(jnp.float32)).astype(jnp.bfloat16)
    weights = jnp.concatenate([a_hi, a_lo], axis=1)
    ga_all[mi] = mtm(a)
    pl.semaphore_wait(barrier, ni + nj + nk - 3)
    ga_cp = [
        remote(ga_all.at[mi], ga_all.at[mi], ga_send.at[d - 1], ga_recv.at[d - 1], peer("ia", mi, ni, d))
        for d in range(1, ni)
    ]

    x_cp, z_cp, p_cp, q_cp = {}, {}, {}, {}
    step = min(256, jb)

    def first(b):
        for k in range(kl):
            tcopies[b, k].wait()

        def chunk(s, carry):
            rs = pl.ds(pl.multiple_of(b * jb + s * step, step), step)
            total = None
            for k in range(kl):
                x = tbuf[k, rs, :]
                hi = x.astype(jnp.bfloat16)
                lo = (x - hi.astype(jnp.float32)).astype(jnp.bfloat16)
                y = jnp.dot(hi, weights, preferred_element_type=jnp.float32) + jnp.dot(
                    lo, weights, preferred_element_type=jnp.float32
                )
                y = y[:, :rank] + y[:, rank:]
                part[k, rs, :] = y
                y = y * c_ref[k : k + 1, :]
                total = y if total is None else total + y
            mloc[rs, :] = total
            return carry

        lax.fori_loop(0, jb // step, chunk, 0)
        for d in range(1, nk):
            other = lax.rem(mk + d, nk)
            rs = pl.ds(pl.multiple_of(b * jb + other * jx, 8), jx)
            x_cp[b, d] = remote(
                mloc.at[rs, :], xrecv.at[b, d - 1], x_send.at[b, d - 1], x_recv.at[b, d - 1],
                peer("ka", mk, nk, d),
            )

    def second(b):
        total = mloc[pl.ds(pl.multiple_of(b * jb + mk * jx, 8), jx), :]
        for d in range(1, nk):
            x_cp[b, d].wait_recv()
            total = total + xrecv[b, d - 1]
        xsum[b] = total
        for d in range(1, ni):
            other = lax.rem(mi + d, ni)
            z_cp[b, d] = remote(
                xsum.at[b, pl.ds(pl.multiple_of(other * jz, 8), jz), :], zrecv.at[b, d - 1],
                z_send.at[b, d - 1], z_recv.at[b, d - 1], peer("ia", mi, ni, d),
            )

    def third(b):
        total = xsum[b, pl.ds(pl.multiple_of(mi * jz, 8), jz), :]
        for d in range(1, ni):
            z_cp[b, d].wait_recv()
            total = total + zrecv[b, d - 1]
        rs = pl.ds(pl.multiple_of(b * jb + mk * jx + mi * jz, 8), jz)
        bfull[rs, :] = mm(total, inv_ref[...])
        for d in range(1, ni):
            p_cp[b, d] = remote(
                bfull.at[rs, :], bfull.at[rs, :], p_send.at[b, d - 1], p_recv.at[b, d - 1],
                peer("ia", mi, ni, d),
            )

    def fourth(b):
        for d in range(1, ni):
            p_cp[b, d].wait_recv()
        rs = pl.ds(pl.multiple_of(b * jb + mk * jx, 8), jx)
        for d in range(1, nk):
            q_cp[b, d] = remote(
                bfull.at[rs, :], bfull.at[rs, :], q_send.at[b, d - 1], q_recv.at[b, d - 1],
                peer("ka", mk, nk, d),
            )

    out_cp = []

    def fifth(b):
        for d in range(1, nk):
            q_cp[b, d].wait_recv()
        rs = pl.ds(b * jb, jb)
        cp = pltpu.make_async_copy(bfull.at[rs, :], b_out.at[rs, :], o_sem.at[b])
        cp.start()
        out_cp.append(cp)
        value = bfull[rs, :]
        acc_ref[pl.ds(0, rank), :] = acc_ref[pl.ds(0, rank), :] + mtm(value)
        for k in range(kl):
            s = jnp.sum(part[k, rs, :] * value, axis=0, keepdims=True)
            acc_ref[pl.ds(rank + k, 1), :] = acc_ref[pl.ds(rank + k, 1), :] + s

    for b in range(blocks):
        first(b)

    for cp in ga_cp:
        cp.wait_recv()
    gram_a = ga_all[0]
    for d in range(1, ni):
        gram_a = gram_a + ga_all[d]
    inv_ref[...] = gram_a * gc_ref[...]
    acc_ref[...] = jnp.zeros_like(acc_ref)
    groups = rank // GROUP
    for b in range(blocks):
        lo, hi = groups * b // blocks, groups * (b + 1) // blocks
        inv_ref[...] = lax.fori_loop(lo, hi, lambda _, v: eliminate(v), inv_ref[...])
        second(b)
    for b in range(blocks + 2):
        if b < blocks:
            third(b)
        if 1 <= b <= blocks:
            fourth(b - 1)
        if b >= 2:
            fifth(b - 2)

    gb_all[mj] = acc_ref[...]
    gb_cp = [
        remote(gb_all.at[mj], gb_all.at[mj], gb_send.at[d - 1], gb_recv.at[d - 1], peer("ja", mj, nj, d))
        for d in range(1, nj)
    ]
    for cp in gb_cp:
        cp.wait_recv()
    total = gb_all[0]
    for d in range(1, nj):
        total = total + gb_all[d]
    mc_all[mi] = total[rank:, :]
    mc_cp = [
        remote(mc_all.at[mi], mc_all.at[mi], mc_send.at[d - 1], mc_recv.at[d - 1], peer("ia", mi, ni, d))
        for d in range(1, ni)
    ]
    gram_a = ga_all[0]
    for d in range(1, ni):
        gram_a = gram_a + ga_all[d]
    inverse = lax.fori_loop(
        0, groups, lambda _, v: eliminate(v), gram_a * total[:rank, :]
    )
    for cp in mc_cp:
        cp.wait_recv()
    mttkrp_c = mc_all[0]
    for d in range(1, ni):
        mttkrp_c = mttkrp_c + mc_all[d]
    c_out[...] = mm(mttkrp_c, inverse)[:kl, :]
    for cp in out_cp:
        cp.wait()
    for cp in sends:
        cp.wait_send()


def body(dims, tensor, factor_a, factor_c, gram_c):
    ni, nj, nk = dims
    rows, kl, il = tensor.shape
    rank = factor_a.shape[1]
    blocks = 4
    jb = rows // blocks
    jx = jb // nk
    jz = jx // ni
    kp = -(-kl // 8) * 8
    f32 = jnp.float32
    dma = pltpu.SemaphoreType.DMA
    vmem = pl.BlockSpec(memory_space=pltpu.VMEM)
    return pl.pallas_call(
        functools.partial(kernel, dims, blocks),
        out_shape=(
            jax.ShapeDtypeStruct((rows, rank), f32),
            jax.ShapeDtypeStruct((kl, rank), f32),
        ),
        in_specs=[pl.BlockSpec(memory_space=pl.ANY), vmem, vmem, vmem],
        out_specs=(pl.BlockSpec(memory_space=pl.ANY), vmem),
        scratch_shapes=[
            pltpu.VMEM((kl, rows, il), f32),
            pltpu.VMEM((kl, rows, rank), f32),
            pltpu.VMEM((rows, rank), f32),
            pltpu.VMEM((blocks, nk - 1, jx, rank), f32),
            pltpu.VMEM((blocks, jx, rank), f32),
            pltpu.VMEM((blocks, ni - 1, jz, rank), f32),
            pltpu.VMEM((rows, rank), f32),
            pltpu.VMEM((ni, rank, rank), f32),
            pltpu.VMEM((nj, rank + kp, rank), f32),
            pltpu.VMEM((ni, kp, rank), f32),
            pltpu.VMEM((rank, rank), f32),
            pltpu.VMEM((rank + kp, rank), f32),
            dma((blocks, kl)),
            dma((blocks, nk - 1)),
            dma((blocks, nk - 1)),
            dma((blocks, ni - 1)),
            dma((blocks, ni - 1)),
            dma((blocks, ni - 1)),
            dma((blocks, ni - 1)),
            dma((blocks, nk - 1)),
            dma((blocks, nk - 1)),
            dma((ni - 1,)),
            dma((ni - 1,)),
            dma((nj - 1,)),
            dma((nj - 1,)),
            dma((ni - 1,)),
            dma((ni - 1,)),
            dma((blocks,)),
        ],
        compiler_params=pltpu.CompilerParams(
            collective_id=0, has_side_effects=True, vmem_limit_bytes=48 * 1024 * 1024
        ),
    )(tensor, factor_a, factor_c, gram_c)


def solution(mesh):
    dims = (mesh.shape["ia"], mesh.shape["ja"], mesh.shape["ka"])
    placed = (P("ja", "ka", "ia"), P("ia", None), P("ka", None), P())
    return jax.shard_map(
        functools.partial(body, dims),
        mesh=mesh,
        in_specs=placed,
        out_specs=(P("ja", None), P("ka", None)),
        check_vma=False,
    )
```

time: 201 us -> 68.9 us (0.34)
  waiting for transfers between devices: 83.7 us -> 0 us
  Pallas kernels: 0 us -> 64.1 us
  other arithmetic: 49.9 us -> 0 us
  blocking collectives: 31.2 us -> 0 us
  matrix products: 20.2 us -> 0 us
  between operations: 13.9 us -> 0.65 us
  local copies, waits for them, and re-layouts: 1.14 us -> 3.97 us
    psum x3 -> x0, waiting for transfers between devices: 83.6 us -> none  [the longest x1 58.4 us: body(): lax.psum(jnp.sum(partial_value * factor_c[None, :, :], axis=1), ('ia', 'k...]
    pallas_call x0 -> x1, Pallas kernels: none -> 64.1 us  [body(): pl.pallas_call(functools.partial(kernel, dims, blocks), out_shape=(jax.Sh...]
    another operation x10 -> x0, other arithmetic: 45.7 us -> none  [the longest x6 24.8 us: right_solve(): lower = jnp.linalg.cholesky(system)]
    psum x1 -> x0, blocking collectives: 31.2 us -> none  [body(): lax.psum(jnp.sum(partial_value * factor_b[:, None, :], axis=0), ('ia', 'j...]
    dot_general x3 -> x0, matrix products: 16 us -> none  [the longest x1 12.6 us: body(): jnp.dot(tensor.reshape(mode_two * mode_three, mode_one), factor_a, precis...]
    another operation x4 -> x0, matrix products: 4.14 us -> none  [the longest x2 2.34 us: right_solve(): lax.linalg.triangular_solve(lower, rhs, left_side=False, lower=True, tran...]
    unnamed x9 -> x8, local copies, waits for them, and re-layouts: 0.96 us -> 3.97 us
    reduce_sum x1 -> x0, other arithmetic: 2.48 us -> none  [body(): jnp.sum(partial_value * factor_b[:, None, :], axis=0)]
  transfers between devices with their start and end apart: 3 -> 0, of which waited for: 2 -> 0; matrix products, arithmetic and copies ran while one was open for 19% -> 0% of each run, Pallas kernels for 0% -> 0%
where the time goes in v1:
time: 68.9 us; the launch traced here: 68.7 us
  Pallas kernels  64.1 us (93%)
  local copies, waits for them, and re-layouts  3.97 us (6%)
    pallas_call x1, Pallas kernels, body(): pl.pallas_call(functools.partial(kernel, dims, blocks), out_shape=(jax.Sh...  64.1 us
    unnamed x8, local copies, waits for them, and re-layouts  3.97 us

profile of v1, /device:TPU:0, one launch (start us, length us, event | category | flops | bytes accessed | tf_op | source)
XLA Modules:
  0.0 68.7 jit_solution(7942900987842230307)
XLA Ops:
  0.6 0.0 copy-start
  0.6 0.9 %copy-done = f32[256,128]{1,0:T(8,128)S(1)} copy-done((f32[256,128]{1,0:T(8,128)S(1)}, f32[256,128]{1,0:T(8,128)}, u32[]{:S(2)}) %copy-start) | copy-done | bytes 131096
  1.5 0.0 copy-start.1
  1.5 0.8 %copy-done.1 = f32[128,128]{1,0:T(8,128)S(1)} copy-done((f32[128,128]{1,0:T(8,128)S(1)}, f32[128,128]{1,0:T(8,128)}, u32[]{:S(2)}) %copy-start.1) | copy-done | bytes 65560
  2.4 0.0 copy-start.2
  2.4 0.7 copy-done.2
  3.1 64.1 %shard_map.59 = (f32[2048,128]{1,0:T(8,128)S(1)}, f32[4,128]{1,0:T(4,128)S(1)}) custom-call(f32[2048,4,256]{2,1,0:T(4,128)} %t_hbm.1, f32[256,128]{1,0:T(8,128)S(1)} %copy-done, f32[4,128]{1,0:T(4,128)S(1)} %copy-done.2, f32[128,128]{1,0:T(8,128)S(1)} %copy-done.1), custom_call_target="tpu_custom_call" | custom-call | tf_op jit(solution)/shard_map/pallas_call | solution.py:274
  67.1 1.0 %copy.8 = f32[2048,128]{1,0:T(8,128)} copy(f32[2048,128]{1,0:T(8,128)S(1)} %get-tuple-element.4) | data formatting | bytes 2097152
  68.1 0.6 copy.9
Async XLA Ops:
  0.6 0.9 %copy-start = (f32[256,128]{1,0:T(8,128)S(1)}, f32[256,128]{1,0:T(8,128)}, u32[]{:S(2)}) copy-start(f32[256,128]{1,0:T(8,128)} %a_ref.1) | copy-start | bytes 393220
  1.5 0.8 %copy-start.1 = (f32[128,128]{1,0:T(8,128)S(1)}, f32[128,128]{1,0:T(8,128)}, u32[]{:S(2)}) copy-start(f32[128,128]{1,0:T(8,128)} %gc_ref.1) | copy-start | bytes 196612
  2.4 0.7 copy-start.2

commit v2 on v1

--- a/solution.py
+++ b/solution.py
@@ -27,22 +27,41 @@
     lane = lax.broadcasted_iota(jnp.int32, (n, n), 1)
     sub = lax.broadcasted_iota(jnp.int32, (n, n), 0)
     lane_row = lax.broadcasted_iota(jnp.int32, (1, n), 1)
-    for t in range(GROUP):
-        col = jnp.broadcast_to(a[:, t : t + 1], (n, n))
-        inv = 1.0 / col[t : t + 1, :]
-        row = jnp.where(lane_row == t, inv, a[t : t + 1, :] * inv)
-        a = jnp.where(sub == t, row, jnp.where(lane == t, 0.0, a) - col * row)
+    for t in range(0, GROUP, 2):
+        c0 = jnp.broadcast_to(a[:, t : t + 1], (n, n))
+        c1 = jnp.broadcast_to(a[:, t + 1 : t + 2], (n, n))
+        p, q = c0[t : t + 1, :], c1[t : t + 1, :]
+        u, s = c0[t + 1 : t + 2, :], c1[t + 1 : t + 2, :]
+        inv = 1.0 / (p * s - q * u)
+        here = lane_row == t
+        there = lane_row == t + 1
+        r0 = jnp.where(here, 1.0, jnp.where(there, 0.0, a[t : t + 1, :]))
+        r1 = jnp.where(here, 0.0, jnp.where(there, 1.0, a[t + 1 : t + 2, :]))
+        w0 = (s * inv) * r0 - (q * inv) * r1
+        w1 = (p * inv) * r1 - (u * inv) * r0
+        base = jnp.where((lane == t) | (lane == t + 1), 0.0, a)
+        base = base - c0 * w0 - c1 * w1
+        a = jnp.where(sub == t, w0, jnp.where(sub == t + 1, w1, base))
     a = pltpu.roll(a, n - GROUP, axis=1)
     return jnp.concatenate([a[GROUP:], a[:GROUP]], axis=0)
+
+
+def scales(h):
+    n = h.shape[0]
+    eye = lax.broadcasted_iota(jnp.int32, (n, n), 1) == lax.broadcasted_iota(jnp.int32, (n, n), 0)
+    kept = jnp.where(eye, h, 0.0)
+    across = lax.rsqrt(jnp.sum(kept, axis=0, keepdims=True))
+    down = lax.rsqrt(jnp.sum(kept, axis=1, keepdims=True))
+    return down, across
 
 
 def kernel(
     dims,
     blocks,
     t_hbm,
-    a_ref,
-    c_ref,
-    gc_ref,
+    a_hbm,
+    c_hbm,
+    gc_hbm,
     b_out,
     c_out,
     tbuf,
@@ -53,10 +72,18 @@
     zrecv,
     bfull,
     ga_all,
-    gb_all,
+    own,
+    g1,
+    g1_in,
+    g2,
+    g3,
+    mj_all,
     mc_all,
     inv_ref,
     acc_ref,
+    a_ref,
+    c_ref,
+    gc_ref,
     t_sem,
     x_send,
     x_recv,
@@ -68,11 +95,18 @@
     q_recv,
     ga_send,
     ga_recv,
-    gb_send,
-    gb_recv,
+    g1_send,
+    g1_recv,
+    g2_send,
+    g2_recv,
+    g3_send,
+    g3_recv,
+    mj_send,
+    mj_recv,
     mc_send,
     mc_recv,
     o_sem,
+    i_sem,
 ):
     ni, nj, nk = dims
     kl, rows, rank = part.shape
@@ -93,6 +127,17 @@
         sends.append(cp)
         return cp
 
+    icopies = []
+    for n, (src, dst) in enumerate(((a_hbm, a_ref), (c_hbm, c_ref), (gc_hbm, gc_ref))):
+        cp = pltpu.make_async_copy(src, dst, i_sem.at[n])
+        cp.start()
+        icopies.append(cp)
+    spot = mk * nj + mj
+
+    def side(e):
+        other = lax.rem(spot + e, nk * nj)
+        return {"ka": lax.div(other, nj), "ja": lax.rem(other, nj)}
+
     tcopies = {}
     for b in range(blocks):
         for k in range(kl):
@@ -102,22 +147,18 @@
             tcopies[b, k] = cp
 
     barrier = pltpu.get_barrier_semaphore()
-    for axis, me, n in (("ia", mi, ni), ("ja", mj, nj), ("ka", mk, nk)):
-        for d in range(1, n):
-            pl.semaphore_signal(
-                barrier, inc=1, device_id=peer(axis, me, n, d), device_id_type=MESH
-            )
-
+    for d in range(1, ni):
+        pl.semaphore_signal(barrier, inc=1, device_id=peer("ia", mi, ni, d), device_id_type=MESH)
+    for e in range(1, nk * nj):
+        pl.semaphore_signal(barrier, inc=1, device_id=side(e), device_id_type=MESH)
+
+    for cp in icopies:
+        cp.wait()
     a = a_ref[...]
     a_hi = a.astype(jnp.bfloat16)
     a_lo = (a - a_hi.astype(jnp.float32)).astype(jnp.bfloat16)
     weights = jnp.concatenate([a_hi, a_lo], axis=1)
     ga_all[mi] = mtm(a)
-    pl.semaphore_wait(barrier, ni + nj + nk - 3)
-    ga_cp = [
-        remote(ga_all.at[mi], ga_all.at[mi], ga_send.at[d - 1], ga_recv.at[d - 1], peer("ia", mi, ni, d))
-        for d in range(1, ni)
-    ]
 
     x_cp, z_cp, p_cp, q_cp = {}, {}, {}, {}
     step = min(256, jb)
@@ -144,6 +185,8 @@
             return carry
 
         lax.fori_loop(0, jb // step, chunk, 0)
+
+    def send_first(b):
         for d in range(1, nk):
             other = lax.rem(mk + d, nk)
             rs = pl.ds(pl.multiple_of(b * jb + other * jx, 8), jx)
@@ -171,7 +214,9 @@
             z_cp[b, d].wait_recv()
             total = total + zrecv[b, d - 1]
         rs = pl.ds(pl.multiple_of(b * jb + mk * jx + mi * jz, 8), jz)
-        bfull[rs, :] = mm(total, inv_ref[...])
+        value = mm(total, inv_ref[...])
+        bfull[rs, :] = value
+        own[pl.ds(b * jz, jz), :] = value
         for d in range(1, ni):
             p_cp[b, d] = remote(
                 bfull.at[rs, :], bfull.at[rs, :], p_send.at[b, d - 1], p_recv.at[b, d - 1],
@@ -198,55 +243,112 @@
         cp.start()
         out_cp.append(cp)
         value = bfull[rs, :]
-        acc_ref[pl.ds(0, rank), :] = acc_ref[pl.ds(0, rank), :] + mtm(value)
         for k in range(kl):
             s = jnp.sum(part[k, rs, :] * value, axis=0, keepdims=True)
-            acc_ref[pl.ds(rank + k, 1), :] = acc_ref[pl.ds(rank + k, 1), :] + s
-
-    for b in range(blocks):
+            acc_ref[pl.ds(k, 1), :] = acc_ref[pl.ds(k, 1), :] + s
+
+    first(0)
+    pl.semaphore_wait(barrier, ni + nk * nj - 2)
+    ga_cp = [
+        remote(ga_all.at[mi], ga_all.at[mi], ga_send.at[d - 1], ga_recv.at[d - 1], peer("ia", mi, ni, d))
+        for d in range(1, ni)
+    ]
+    send_first(0)
+    for b in range(1, blocks):
         first(b)
-
+        send_first(b)
+
+    acc_ref[...] = jnp.zeros_like(acc_ref)
     for cp in ga_cp:
         cp.wait_recv()
     gram_a = ga_all[0]
     for d in range(1, ni):
         gram_a = gram_a + ga_all[d]
-    inv_ref[...] = gram_a * gc_ref[...]
-    acc_ref[...] = jnp.zeros_like(acc_ref)
     groups = rank // GROUP
+
+    def turn(h, quarter):
+        lo, hi = groups * quarter // 4, groups * (quarter + 1) // 4
+        return lax.fori_loop(lo, hi, lambda _, v: eliminate(v), h)
+
+    h = gram_a * gc_ref[...]
+    down, across = scales(h)
+    h = h * down * across
+    at = 0
+    for quarter in range(4):
+        h = turn(h, quarter)
+        while at < blocks * (quarter + 1) // 4:
+            second(at)
+            at += 1
+    inv_ref[...] = h * down * across
     for b in range(blocks):
-        lo, hi = groups * b // blocks, groups * (b + 1) // blocks
-        inv_ref[...] = lax.fori_loop(lo, hi, lambda _, v: eliminate(v), inv_ref[...])
-        second(b)
-    for b in range(blocks + 2):
-        if b < blocks:
-            third(b)
-        if 1 <= b <= blocks:
+        third(b)
+        if b >= 1:
             fourth(b - 1)
-        if b >= 2:
-            fifth(b - 2)
-
-    gb_all[mj] = acc_ref[...]
-    gb_cp = [
-        remote(gb_all.at[mj], gb_all.at[mj], gb_send.at[d - 1], gb_recv.at[d - 1], peer("ja", mj, nj, d))
+
+    cut = rank // ni if rank % (8 * ni) == 0 else rank
+    split = cut != rank
+    g1[...] = mtm(own[...])
+    mine = pl.ds(pl.multiple_of(mi * cut, 8), cut) if split else pl.ds(0, rank)
+    g1_in[mi] = g1[mine, :]
+    g1_cp = []
+    for d in range(1, ni):
+        other = lax.rem(mi + d, ni)
+        rs = pl.ds(pl.multiple_of(other * cut, 8), cut) if split else pl.ds(0, rank)
+        g1_cp.append(
+            remote(g1.at[rs, :], g1_in.at[mi], g1_send.at[d - 1], g1_recv.at[d - 1], peer("ia", mi, ni, d))
+        )
+    fourth(blocks - 1)
+    for cp in g1_cp:
+        cp.wait_recv()
+    total = g1_in[0]
+    for d in range(1, ni):
+        total = total + g1_in[d]
+    g2[spot] = total
+    g2_cp = [
+        remote(g2.at[spot], g2.at[spot], g2_send.at[e - 1], g2_recv.at[e - 1], side(e))
+        for e in range(1, nk * nj)
+    ]
+    half = blocks // 2
+    for b in range(half):
+        fifth(b)
+    for cp in g2_cp:
+        cp.wait_recv()
+    total = g2[0]
+    for e in range(1, nk * nj):
+        total = total + g2[e]
+    g3[mine, :] = total
+    g3_cp = []
+    if split:
+        g3_cp = [
+            remote(g3.at[mine, :], g3.at[mine, :], g3_send.at[d - 1], g3_recv.at[d - 1], peer("ia", mi, ni, d))
+            for d in range(1, ni)
+        ]
+    for b in range(half, blocks - 1):
+        fifth(b)
+    for cp in g3_cp:
+        cp.wait_recv()
+    h = gram_a * g3[...]
+    down, across = scales(h)
+    h = turn(h * down * across, 0)
+    fifth(blocks - 1)
+    mj_all[mj] = acc_ref[...]
+    mj_cp = [
+        remote(mj_all.at[mj], mj_all.at[mj], mj_send.at[d - 1], mj_recv.at[d - 1], peer("ja", mj, nj, d))
         for d in range(1, nj)
     ]
-    for cp in gb_cp:
-        cp.wait_recv()
-    total = gb_all[0]
+    h = turn(h, 1)
+    for cp in mj_cp:
+        cp.wait_recv()
+    total = mj_all[0]
     for d in range(1, nj):
-        total = total + gb_all[d]
-    mc_all[mi] = total[rank:, :]
+        total = total + mj_all[d]
+    mc_all[mi] = total
     mc_cp = [
         remote(mc_all.at[mi], mc_all.at[mi], mc_send.at[d - 1], mc_recv.at[d - 1], peer("ia", mi, ni, d))
         for d in range(1, ni)
     ]
-    gram_a = ga_all[0]
-    for d in range(1, ni):
-        gram_a = gram_a + ga_all[d]
-    inverse = lax.fori_loop(
-        0, groups, lambda _, v: eliminate(v), gram_a * total[:rank, :]
-    )
+    h = turn(turn(h, 2), 3)
+    inverse = h * down * across
     for cp in mc_cp:
         cp.wait_recv()
     mttkrp_c = mc_all[0]
@@ -268,6 +370,7 @@
     jx = jb // nk
     jz = jx // ni
     kp = -(-kl // 8) * 8
+    cut = rank // ni if rank % (8 * ni) == 0 else rank
     f32 = jnp.float32
     dma = pltpu.SemaphoreType.DMA
     vmem = pl.BlockSpec(memory_space=pltpu.VMEM)
@@ -277,7 +380,7 @@
             jax.ShapeDtypeStruct((rows, rank), f32),
             jax.ShapeDtypeStruct((kl, rank), f32),
         ),
-        in_specs=[pl.BlockSpec(memory_space=pl.ANY), vmem, vmem, vmem],
+        in_specs=[pl.BlockSpec(memory_space=pltpu.HBM)] * 4,
         out_specs=(pl.BlockSpec(memory_space=pl.ANY), vmem),
         scratch_shapes=[
             pltpu.VMEM((kl, rows, il), f32),
@@ -288,10 +391,18 @@
             pltpu.VMEM((blocks, ni - 1, jz, rank), f32),
             pltpu.VMEM((rows, rank), f32),
             pltpu.VMEM((ni, rank, rank), f32),
-            pltpu.VMEM((nj, rank + kp, rank), f32),
+            pltpu.VMEM((blocks * jz, rank), f32),
+            pltpu.VMEM((rank, rank), f32),
+            pltpu.VMEM((ni, cut, rank), f32),
+            pltpu.VMEM((nk * nj, cut, rank), f32),
+            pltpu.VMEM((rank, rank), f32),
+            pltpu.VMEM((nj, kp, rank), f32),
             pltpu.VMEM((ni, kp, rank), f32),
             pltpu.VMEM((rank, rank), f32),
-            pltpu.VMEM((rank + kp, rank), f32),
+            pltpu.VMEM((kp, rank), f32),
+            pltpu.VMEM((il, rank), f32),
+            pltpu.VMEM((kl, rank), f32),
+            pltpu.VMEM((rank, rank), f32),
             dma((blocks, kl)),
             dma((blocks, nk - 1)),
             dma((blocks, nk - 1)),
@@ -303,11 +414,18 @@
             dma((blocks, nk - 1)),
             dma((ni - 1,)),
             dma((ni - 1,)),
+            dma((ni - 1,)),
+            dma((ni - 1,)),
+            dma((nk * nj - 1,)),
+            dma((nk * nj - 1,)),
+            dma((ni - 1,)),
+            dma((ni - 1,)),
             dma((nj - 1,)),
             dma((nj - 1,)),
             dma((ni - 1,)),
             dma((ni - 1,)),
             dma((blocks,)),
+            dma((3,)),
         ],
         compiler_params=pltpu.CompilerParams(
             collective_id=0, has_side_effects=True, vmem_limit_bytes=48 * 1024 * 1024

time: 68.9 us -> 65.1 us (0.945)
  Pallas kernels: 64.1 us -> 60.3 us
    pallas_call x1, Pallas kernels: 64.1 us -> 60.3 us  [body(): pl.pallas_call(functools.partial(kernel, dims, blocks), out_shape=(jax.Sh...]
where the time goes in v2:
time: 65.1 us; the launch traced here: 64.9 us
  Pallas kernels  60.3 us (93%)
  local copies, waits for them, and re-layouts  3.97 us (6%)
    pallas_call x1, Pallas kernels, body(): pl.pallas_call(functools.partial(kernel, dims, blocks), out_shape=(jax.Sh...  60.3 us
    unnamed x8, local copies, waits for them, and re-layouts  3.97 us

profile of v2, /device:TPU:0, one launch (start us, length us, event | category | flops | bytes accessed | tf_op | source)
XLA Modules:
  0.0 64.9 jit_solution(1592649924570529770)
XLA Ops:
  0.6 0.0 copy-start
  0.6 0.9 %copy-done = f32[256,128]{1,0:T(8,128)S(1)} copy-done((f32[256,128]{1,0:T(8,128)S(1)}, f32[256,128]{1,0:T(8,128)}, u32[]{:S(2)}) %copy-start) | copy-done | bytes 131096
  1.5 0.0 copy-start.1
  1.5 0.8 %copy-done.1 = f32[128,128]{1,0:T(8,128)S(1)} copy-done((f32[128,128]{1,0:T(8,128)S(1)}, f32[128,128]{1,0:T(8,128)}, u32[]{:S(2)}) %copy-start.1) | copy-done | bytes 65560
  2.4 0.0 copy-start.2
  2.4 0.7 %copy-done.2 = f32[4,128]{1,0:T(4,128)S(1)} copy-done((f32[4,128]{1,0:T(4,128)S(1)}, f32[4,128]{1,0:T(4,128)}, u32[]{:S(2)}) %copy-start.2) | copy-done | bytes 2072
  3.1 60.3 %shard_map.59 = (f32[2048,128]{1,0:T(8,128)S(1)}, f32[4,128]{1,0:T(4,128)S(1)}) custom-call(f32[2048,4,256]{2,1,0:T(4,128)} %t_hbm.1, f32[256,128]{1,0:T(8,128)S(1)} %copy-done, f32[4,128]{1,0:T(4,128)S(1)} %copy-done.2, f32[128,128]{1,0:T(8,128)S(1)} %copy-done.1), custom_call_target="tpu_custom_call" | custom-call | tf_op jit(solution)/shard_map/pallas_call | solution.py:377
  63.4 1.0 %copy.8 = f32[2048,128]{1,0:T(8,128)} copy(f32[2048,128]{1,0:T(8,128)S(1)} %get-tuple-element.4) | data formatting | bytes 2097152
  64.3 0.6 copy.9
Async XLA Ops:
  0.6 0.9 %copy-start = (f32[256,128]{1,0:T(8,128)S(1)}, f32[256,128]{1,0:T(8,128)}, u32[]{:S(2)}) copy-start(f32[256,128]{1,0:T(8,128)} %a_hbm.1) | copy-start | bytes 393220
  1.5 0.8 %copy-start.1 = (f32[128,128]{1,0:T(8,128)S(1)}, f32[128,128]{1,0:T(8,128)}, u32[]{:S(2)}) copy-start(f32[128,128]{1,0:T(8,128)} %gc_hbm.1) | copy-start | bytes 196612
  2.4 0.7 %copy-start.2 = (f32[4,128]{1,0:T(4,128)S(1)}, f32[4,128]{1,0:T(4,128)}, u32[]{:S(2)}) copy-start(f32[4,128]{1,0:T(4,128)} %c_hbm.1) | copy-start | bytes 6148

commit v3 on v2

--- a/solution.py
+++ b/solution.py
@@ -9,7 +9,7 @@
 
 HIGH = lax.Precision.HIGHEST
 MESH = pl.DeviceIdType.MESH
-GROUP = 8
+GROUP = 16
 
 
 def mm(a, b):
@@ -71,11 +71,11 @@
     xsum,
     zrecv,
     bfull,
-    ga_all,
-    own,
+    ga_loc,
+    ga_in,
+    ga_full,
     g1,
     g1_in,
-    g2,
     g3,
     mj_all,
     mc_all,
@@ -95,10 +95,10 @@
     q_recv,
     ga_send,
     ga_recv,
+    gf_send,
+    gf_recv,
     g1_send,
     g1_recv,
-    g2_send,
-    g2_recv,
     g3_send,
     g3_recv,
     mj_send,
@@ -132,12 +132,6 @@
         cp = pltpu.make_async_copy(src, dst, i_sem.at[n])
         cp.start()
         icopies.append(cp)
-    spot = mk * nj + mj
-
-    def side(e):
-        other = lax.rem(spot + e, nk * nj)
-        return {"ka": lax.div(other, nj), "ja": lax.rem(other, nj)}
-
     tcopies = {}
     for b in range(blocks):
         for k in range(kl):
@@ -149,8 +143,10 @@
     barrier = pltpu.get_barrier_semaphore()
     for d in range(1, ni):
         pl.semaphore_signal(barrier, inc=1, device_id=peer("ia", mi, ni, d), device_id_type=MESH)
-    for e in range(1, nk * nj):
-        pl.semaphore_signal(barrier, inc=1, device_id=side(e), device_id_type=MESH)
+    for d in range(1, nj):
+        pl.semaphore_signal(barrier, inc=1, device_id=peer("ja", mj, nj, d), device_id_type=MESH)
+    for d in range(1, nk):
+        pl.semaphore_signal(barrier, inc=1, device_id=peer("ka", mk, nk, d), device_id_type=MESH)
 
     for cp in icopies:
         cp.wait()
@@ -158,7 +154,7 @@
     a_hi = a.astype(jnp.bfloat16)
     a_lo = (a - a_hi.astype(jnp.float32)).astype(jnp.bfloat16)
     weights = jnp.concatenate([a_hi, a_lo], axis=1)
-    ga_all[mi] = mtm(a)
+    ga_loc[...] = mtm(a)
 
     x_cp, z_cp, p_cp, q_cp = {}, {}, {}, {}
     step = min(256, jb)
@@ -195,37 +191,66 @@
                 peer("ka", mk, nk, d),
             )
 
+    hops = []
+    while 2 ** len(hops) < ni:
+        hops.append(2 ** len(hops))
+    levels = len(hops)
+    bits = [lax.rem(lax.div(mi, m), 2) for m in hops]
+    starts, arrive = [0], [0]
+    for n in range(levels):
+        starts.append(starts[n] + bits[n] * (jx >> (n + 1)))
+        arrive.append(arrive[n] + (jx >> (n + 1)))
+
+    def across_ia(n):
+        return {"ia": mi + hops[n] * (1 - 2 * bits[n])}
+
+    def z_start(b, n):
+        size = jx >> (n + 1)
+        give = pl.ds(pl.multiple_of(starts[n] + (1 - bits[n]) * size, 8), size)
+        z_cp[b, n] = remote(
+            xsum.at[b, give, :], zrecv.at[b, pl.ds(arrive[n], size), :], z_send.at[b, n],
+            z_recv.at[b, n], across_ia(n),
+        )
+
+    def z_finish(b, n):
+        size = jx >> (n + 1)
+        z_cp[b, n].wait_recv()
+        keep = pl.ds(pl.multiple_of(starts[n + 1], 8), size)
+        return keep, xsum[b, keep, :] + zrecv[b, pl.ds(arrive[n], size), :]
+
+    def p_start(b, n):
+        rs = pl.ds(pl.multiple_of(b * jb + mk * jx + starts[n + 1], 8), jx >> (n + 1))
+        p_cp[b, n] = remote(
+            bfull.at[rs, :], bfull.at[rs, :], p_send.at[b, n], p_recv.at[b, n], across_ia(n)
+        )
+
     def second(b):
         total = mloc[pl.ds(pl.multiple_of(b * jb + mk * jx, 8), jx), :]
         for d in range(1, nk):
             x_cp[b, d].wait_recv()
             total = total + xrecv[b, d - 1]
         xsum[b] = total
-        for d in range(1, ni):
-            other = lax.rem(mi + d, ni)
-            z_cp[b, d] = remote(
-                xsum.at[b, pl.ds(pl.multiple_of(other * jz, 8), jz), :], zrecv.at[b, d - 1],
-                z_send.at[b, d - 1], z_recv.at[b, d - 1], peer("ia", mi, ni, d),
-            )
+        z_start(b, 0)
+
+    def reduce_more(b):
+        for n in range(levels - 1):
+            keep, value = z_finish(b, n)
+            xsum[b, keep, :] = value
+            z_start(b, n + 1)
 
     def third(b):
-        total = xsum[b, pl.ds(pl.multiple_of(mi * jz, 8), jz), :]
-        for d in range(1, ni):
-            z_cp[b, d].wait_recv()
-            total = total + zrecv[b, d - 1]
-        rs = pl.ds(pl.multiple_of(b * jb + mk * jx + mi * jz, 8), jz)
-        value = mm(total, inv_ref[...])
-        bfull[rs, :] = value
-        own[pl.ds(b * jz, jz), :] = value
-        for d in range(1, ni):
-            p_cp[b, d] = remote(
-                bfull.at[rs, :], bfull.at[rs, :], p_send.at[b, d - 1], p_recv.at[b, d - 1],
-                peer("ia", mi, ni, d),
-            )
+        _, total = z_finish(b, levels - 1)
+        rs = pl.ds(pl.multiple_of(b * jb + mk * jx + starts[levels], 8), jz)
+        bfull[rs, :] = mm(total, inv_ref[...])
+        p_start(b, levels - 1)
+
+    def gather_more(b):
+        for n in range(levels - 1, 0, -1):
+            p_cp[b, n].wait_recv()
+            p_start(b, n - 1)
 
     def fourth(b):
-        for d in range(1, ni):
-            p_cp[b, d].wait_recv()
+        p_cp[b, 0].wait_recv()
         rs = pl.ds(pl.multiple_of(b * jb + mk * jx, 8), jx)
         for d in range(1, nk):
             q_cp[b, d] = remote(
@@ -243,27 +268,49 @@
         cp.start()
         out_cp.append(cp)
         value = bfull[rs, :]
+        g1[...] = g1[...] + mtm(value)
         for k in range(kl):
             s = jnp.sum(part[k, rs, :] * value, axis=0, keepdims=True)
             acc_ref[pl.ds(k, 1), :] = acc_ref[pl.ds(k, 1), :] + s
 
     first(0)
-    pl.semaphore_wait(barrier, ni + nk * nj - 2)
+    pl.semaphore_wait(barrier, ni + nj + nk - 3)
+    strip = rank // nj
+    part_rows = pl.ds(pl.multiple_of(mj * strip, 8), strip)
+    ga_in[mi] = ga_loc[part_rows, :]
     ga_cp = [
-        remote(ga_all.at[mi], ga_all.at[mi], ga_send.at[d - 1], ga_recv.at[d - 1], peer("ia", mi, ni, d))
+        remote(
+            ga_loc.at[part_rows, :], ga_in.at[mi], ga_send.at[d - 1], ga_recv.at[d - 1],
+            peer("ia", mi, ni, d),
+        )
         for d in range(1, ni)
     ]
     send_first(0)
+    gf_cp = []
     for b in range(1, blocks):
         first(b)
         send_first(b)
+        if b == min(2, blocks - 1):
+            for cp in ga_cp:
+                cp.wait_recv()
+            total = ga_in[0]
+            for d in range(1, ni):
+                total = total + ga_in[d]
+            ga_full[part_rows, :] = total
+            for d in range(1, nj):
+                gf_cp.append(
+                    remote(
+                        ga_full.at[part_rows, :], ga_full.at[part_rows, :], gf_send.at[d - 1],
+                        gf_recv.at[d - 1], peer("ja", mj, nj, d),
+                    )
+                )
 
     acc_ref[...] = jnp.zeros_like(acc_ref)
-    for cp in ga_cp:
+    g1[...] = jnp.zeros_like(g1)
+    second(0)
+    for cp in gf_cp:
         cp.wait_recv()
-    gram_a = ga_all[0]
-    for d in range(1, ni):
-        gram_a = gram_a + ga_all[d]
+    gram_a = ga_full[...]
     groups = rank // GROUP
 
     def turn(h, quarter):
@@ -273,70 +320,45 @@
     h = gram_a * gc_ref[...]
     down, across = scales(h)
     h = h * down * across
-    at = 0
-    for quarter in range(4):
-        h = turn(h, quarter)
-        while at < blocks * (quarter + 1) // 4:
-            second(at)
-            at += 1
+    h = turn(turn(h, 0), 1)
+    second(1)
+    reduce_more(0)
+    h = turn(turn(h, 2), 3)
     inv_ref[...] = h * down * across
-    for b in range(blocks):
-        third(b)
-        if b >= 1:
-            fourth(b - 1)
-
-    cut = rank // ni if rank % (8 * ni) == 0 else rank
-    split = cut != rank
-    g1[...] = mtm(own[...])
-    mine = pl.ds(pl.multiple_of(mi * cut, 8), cut) if split else pl.ds(0, rank)
-    g1_in[mi] = g1[mine, :]
+    stages = (second, reduce_more, third, gather_more, fourth, fifth)
+    done = [2, 1, 0, 0, 0, 0]
+    while done[5] < blocks:
+        for n in range(6):
+            if done[n] < (blocks if n == 0 else before[n - 1]):
+                stages[n](done[n])
+                done[n] += 1
+            if n == 0:
+                before = list(done)
+
+    cut = rank // nj
+    mine = pl.ds(pl.multiple_of(mj * cut, 8), cut)
+    g1_in[mj] = g1[mine, :]
     g1_cp = []
-    for d in range(1, ni):
-        other = lax.rem(mi + d, ni)
-        rs = pl.ds(pl.multiple_of(other * cut, 8), cut) if split else pl.ds(0, rank)
+    for d in range(1, nj):
+        rs = pl.ds(pl.multiple_of(lax.rem(mj + d, nj) * cut, 8), cut)
         g1_cp.append(
-            remote(g1.at[rs, :], g1_in.at[mi], g1_send.at[d - 1], g1_recv.at[d - 1], peer("ia", mi, ni, d))
+            remote(g1.at[rs, :], g1_in.at[mj], g1_send.at[d - 1], g1_recv.at[d - 1], peer("ja", mj, nj, d))
         )
-    fourth(blocks - 1)
-    for cp in g1_cp:
-        cp.wait_recv()
-    total = g1_in[0]
-    for d in range(1, ni):
-        total = total + g1_in[d]
-    g2[spot] = total
-    g2_cp = [
-        remote(g2.at[spot], g2.at[spot], g2_send.at[e - 1], g2_recv.at[e - 1], side(e))
-        for e in range(1, nk * nj)
-    ]
-    half = blocks // 2
-    for b in range(half):
-        fifth(b)
-    for cp in g2_cp:
-        cp.wait_recv()
-    total = g2[0]
-    for e in range(1, nk * nj):
-        total = total + g2[e]
-    g3[mine, :] = total
-    g3_cp = []
-    if split:
-        g3_cp = [
-            remote(g3.at[mine, :], g3.at[mine, :], g3_send.at[d - 1], g3_recv.at[d - 1], peer("ia", mi, ni, d))
-            for d in range(1, ni)
-        ]
-    for b in range(half, blocks - 1):
-        fifth(b)
-    for cp in g3_cp:
-        cp.wait_recv()
-    h = gram_a * g3[...]
-    down, across = scales(h)
-    h = turn(h * down * across, 0)
-    fifth(blocks - 1)
     mj_all[mj] = acc_ref[...]
     mj_cp = [
         remote(mj_all.at[mj], mj_all.at[mj], mj_send.at[d - 1], mj_recv.at[d - 1], peer("ja", mj, nj, d))
         for d in range(1, nj)
     ]
-    h = turn(h, 1)
+    for cp in g1_cp:
+        cp.wait_recv()
+    total = g1_in[0]
+    for d in range(1, nj):
+        total = total + g1_in[d]
+    g3[mine, :] = total
+    g3_cp = [
+        remote(g3.at[mine, :], g3.at[mine, :], g3_send.at[d - 1], g3_recv.at[d - 1], peer("ja", mj, nj, d))
+        for d in range(1, nj)
+    ]
     for cp in mj_cp:
         cp.wait_recv()
     total = mj_all[0]
@@ -347,7 +369,13 @@
         remote(mc_all.at[mi], mc_all.at[mi], mc_send.at[d - 1], mc_recv.at[d - 1], peer("ia", mi, ni, d))
         for d in range(1, ni)
     ]
-    h = turn(turn(h, 2), 3)
+    for cp in g3_cp:
+        cp.wait_recv()
+    h = gram_a * g3[...]
+    down, across = scales(h)
+    h = h * down * across
+    for quarter in range(4):
+        h = turn(h, quarter)
     inverse = h * down * across
     for cp in mc_cp:
         cp.wait_recv()
@@ -370,7 +398,8 @@
     jx = jb // nk
     jz = jx // ni
     kp = -(-kl // 8) * 8
-    cut = rank // ni if rank % (8 * ni) == 0 else rank
+    hops = (ni - 1).bit_length()
+    strip = rank // nj
     f32 = jnp.float32
     dma = pltpu.SemaphoreType.DMA
     vmem = pl.BlockSpec(memory_space=pltpu.VMEM)
@@ -388,13 +417,13 @@
             pltpu.VMEM((rows, rank), f32),
             pltpu.VMEM((blocks, nk - 1, jx, rank), f32),
             pltpu.VMEM((blocks, jx, rank), f32),
-            pltpu.VMEM((blocks, ni - 1, jz, rank), f32),
+            pltpu.VMEM((blocks, jx, rank), f32),
             pltpu.VMEM((rows, rank), f32),
-            pltpu.VMEM((ni, rank, rank), f32),
-            pltpu.VMEM((blocks * jz, rank), f32),
-            pltpu.VMEM((rank, rank), f32),
-            pltpu.VMEM((ni, cut, rank), f32),
-            pltpu.VMEM((nk * nj, cut, rank), f32),
+            pltpu.VMEM((rank, rank), f32),
+            pltpu.VMEM((ni, strip, rank), f32),
+            pltpu.VMEM((rank, rank), f32),
+            pltpu.VMEM((rank, rank), f32),
+            pltpu.VMEM((nj, rank // nj, rank), f32),
             pltpu.VMEM((rank, rank), f32),
             pltpu.VMEM((nj, kp, rank), f32),
             pltpu.VMEM((ni, kp, rank), f32),
@@ -406,20 +435,20 @@
             dma((blocks, kl)),
             dma((blocks, nk - 1)),
             dma((blocks, nk - 1)),
-            dma((blocks, ni - 1)),
-            dma((blocks, ni - 1)),
-            dma((blocks, ni - 1)),
-            dma((blocks, ni - 1)),
+            dma((blocks, hops)),
+            dma((blocks, hops)),
+            dma((blocks, hops)),
+            dma((blocks, hops)),
             dma((blocks, nk - 1)),
             dma((blocks, nk - 1)),
             dma((ni - 1,)),
             dma((ni - 1,)),
-            dma((ni - 1,)),
-            dma((ni - 1,)),
-            dma((nk * nj - 1,)),
-            dma((nk * nj - 1,)),
-            dma((ni - 1,)),
-            dma((ni - 1,)),
+            dma((nj - 1,)),
+            dma((nj - 1,)),
+            dma((nj - 1,)),
+            dma((nj - 1,)),
+            dma((nj - 1,)),
+            dma((nj - 1,)),
             dma((nj - 1,)),
             dma((nj - 1,)),
             dma((ni - 1,)),

time: 65.1 us -> 62.5 us (0.960)
  Pallas kernels: 60.3 us -> 57.7 us
    pallas_call x1, Pallas kernels: 60.3 us -> 57.7 us  [body(): pl.pallas_call(functools.partial(kernel, dims, blocks), out_shape=(jax.Sh...]
where the time goes in v3:
time: 62.5 us; the launch traced here: 62.3 us
  Pallas kernels  57.7 us (92%)
  local copies, waits for them, and re-layouts  3.97 us (6%)
  between operations  0.65 us (1%)
    pallas_call x1, Pallas kernels, body(): pl.pallas_call(functools.partial(kernel, dims, blocks), out_shape=(jax.Sh...  57.7 us
    unnamed x8, local copies, waits for them, and re-layouts  3.97 us

profile of v3, /device:TPU:0, one launch (start us, length us, event | category | flops | bytes accessed | tf_op | source)
XLA Modules:
  0.0 62.3 jit_solution(6964342248790791333)
XLA Ops:
  0.6 0.0 copy-start
  0.6 0.9 %copy-done = f32[256,128]{1,0:T(8,128)S(1)} copy-done((f32[256,128]{1,0:T(8,128)S(1)}, f32[256,128]{1,0:T(8,128)}, u32[]{:S(2)}) %copy-start) | copy-done | bytes 131096
  1.5 0.0 copy-start.1
  1.5 0.8 %copy-done.1 = f32[128,128]{1,0:T(8,128)S(1)} copy-done((f32[128,128]{1,0:T(8,128)S(1)}, f32[128,128]{1,0:T(8,128)}, u32[]{:S(2)}) %copy-start.1) | copy-done | bytes 65560
  2.4 0.0 copy-start.2
  2.4 0.7 %copy-done.2 = f32[4,128]{1,0:T(4,128)S(1)} copy-done((f32[4,128]{1,0:T(4,128)S(1)}, f32[4,128]{1,0:T(4,128)}, u32[]{:S(2)}) %copy-start.2) | copy-done | bytes 2072
  3.1 57.7 %shard_map.59 = (f32[2048,128]{1,0:T(8,128)S(1)}, f32[4,128]{1,0:T(4,128)S(1)}) custom-call(f32[2048,4,256]{2,1,0:T(4,128)} %t_hbm.1, f32[256,128]{1,0:T(8,128)S(1)} %copy-done, f32[4,128]{1,0:T(4,128)S(1)} %copy-done.2, f32[128,128]{1,0:T(8,128)S(1)} %copy-done.1), custom_call_target="tpu_custom_call" | custom-call | tf_op jit(solution)/shard_map/pallas_call | solution.py:406
  60.8 1.0 %copy.8 = f32[2048,128]{1,0:T(8,128)} copy(f32[2048,128]{1,0:T(8,128)S(1)} %get-tuple-element.4) | data formatting | bytes 2097152
  61.7 0.6 copy.9
Async XLA Ops:
  0.6 0.9 %copy-start = (f32[256,128]{1,0:T(8,128)S(1)}, f32[256,128]{1,0:T(8,128)}, u32[]{:S(2)}) copy-start(f32[256,128]{1,0:T(8,128)} %a_hbm.1) | copy-start | bytes 393220
  1.5 0.8 %copy-start.1 = (f32[128,128]{1,0:T(8,128)S(1)}, f32[128,128]{1,0:T(8,128)}, u32[]{:S(2)}) copy-start(f32[128,128]{1,0:T(8,128)} %gc_hbm.1) | copy-start | bytes 196612
  2.4 0.7 %copy-start.2 = (f32[4,128]{1,0:T(4,128)S(1)}, f32[4,128]{1,0:T(4,128)}, u32[]{:S(2)}) copy-start(f32[4,128]{1,0:T(4,128)} %c_hbm.1) | copy-start | bytes 6148
